TPU v7x, 256 devices: a whole 4x4x8 slice. The times are simulated.
256 devices in a mesh: expert: 64 (over y_hi, x, z), half: 2 (over y_lo), dp: 2 (over core).
Axes of the slice: x: 4, y: 4 (y_hi: 2, y_lo: 2; y = y_hi * 2 + y_lo), z: 8, core: 2. Of those that a mesh axis runs over, the one named last changes fastest.
Arguments:
- tokens: bfloat16 [16384, 4096], P(('expert', 'dp'), 'half'), may hold values from -6 to 6
- cotangent: bfloat16 [16384, 4096], P(('expert', 'dp'), 'half'), may hold values from -12 to 12
- expert_ids: int32 [16384, 8], P(('expert', 'dp')), may hold values from 0 to 63, as said below
- slot_ids: int32 [16384, 8], P(('expert', 'dp')), may hold values from 0 to 17, as said below
- gate_weights: float32 [16384, 8], P(('expert', 'dp')), may hold values from 0.03 to 0.4
- latent_down: bfloat16 [4096, 1024], P('half', 'dp'), may hold values from -0.09375 to 0.09375
- latent_up: bfloat16 [1024, 4096], P('dp', 'half'), may hold values from -0.1875 to 0.1875
- expert_gate: bfloat16 [64, 1024, 1536], P('expert', 'dp', 'half'), may hold values from -0.1875 to 0.1875
- expert_linear: bfloat16 [64, 1024, 1536], P('expert', 'dp', 'half'), may hold values from -0.1875 to 0.1875
- expert_out: bfloat16 [64, 1536, 1024], P('expert', 'half', 'dp'), may hold values from -0.15625 to 0.15625
Outputs:
- token_grad: bfloat16 [16384, 4096], P(('expert', 'dp'), 'half')
- gate_grad: bfloat16 [64, 1024, 1536], P('expert', 'dp', 'half')
- linear_grad: bfloat16 [64, 1024, 1536], P('expert', 'dp', 'half')
- out_grad: bfloat16 [64, 1536, 1024], P('expert', 'half', 'dp')
Inputs may be any that keep to these rules, and one draw needn't show every extreme that they name: `expert_ids`: each row names 8 different experts. In each aligned block of 128 rows (the rows of one device) no expert is named by more than 18 rows, and one expert is named by exactly 18 rows in every block. `slot_ids`: within one aligned block of 128 rows, the entries that name the same expert have different slots.
All inputs are finite; a program needn't handle non-finite values.
Results may differ from a plain program's by a relative error of at most 0.013.
Values may be sent and summed in bfloat16 or wider, within the bound.
A program may use at most 128 MiB of HBM per device.

v0:
```python
import jax
import jax.numpy as jnp
from jax import lax
from jax.sharding import PartitionSpec as P


def on_device(
    tokens,
    cotangent,
    expert_ids,
    slot_ids,
    gate_weights,
    latent_down,
    latent_up,
    expert_gate,
    expert_linear,
    expert_out,
):
    row_count = tokens.shape[0]
    pick_count = expert_ids.shape[1]
    local_count = expert_gate.shape[0]
    group_count = lax.axis_size("expert")
    expert_count = group_count * local_count
    capacity = min(
        row_count, 2 * ((9 * row_count * pick_count + 16 * expert_count - 1) // (16 * expert_count))
    )
    down_full, up_full, gate_full, linear_full, output_full = (
        lax.all_gather(latent_down, "dp", axis=1, tiled=True),
        lax.all_gather(latent_up, "dp", axis=0, tiled=True),
        lax.all_gather(expert_gate, "dp", axis=1, tiled=True),
        lax.all_gather(expert_linear, "dp", axis=1, tiled=True),
        lax.all_gather(expert_out, "dp", axis=2, tiled=True),
    )
    latent_part = jnp.dot(tokens, down_full, preferred_element_type=jnp.float32)
    back_part = lax.dot_general(
        cotangent, up_full, (((1,), (1,)), ((), ())), preferred_element_type=jnp.float32
    )
    latent_sum, back_latent = lax.psum((latent_part, back_part), "half")
    latent = latent_sum.astype(jnp.bfloat16)
    width = latent.shape[1]
    flat_slot = (expert_ids * capacity + slot_ids).reshape(-1)
    slot_table = lax.broadcasted_iota(
        jnp.int32, (expert_count * capacity, row_count * pick_count), 0
    )
    matches = flat_slot[None, :] == slot_table
    choice_index = lax.broadcasted_iota(jnp.int32, matches.shape, 1)
    source = jnp.sum(jnp.where(matches, choice_index, 0), axis=1)
    filled = jnp.any(matches, axis=1)
    token_of = source // pick_count
    gate_of = gate_weights.reshape(-1)[source]
    send_latent = jnp.where(filled[:, None], latent[token_of], jnp.zeros((), jnp.bfloat16))
    send_back = jnp.where(filled[:, None], gate_of[:, None] * back_latent[token_of], 0.0).astype(
        jnp.bfloat16
    )
    send_latent = send_latent.reshape(group_count, local_count, capacity, width)
    send_back = send_back.reshape(group_count, local_count, capacity, width)
    rows_latent, rows_back = (
        lax.all_to_all(send_latent, "expert", split_axis=0, concat_axis=0, tiled=True),
        lax.all_to_all(send_back, "expert", split_axis=0, concat_axis=0, tiled=True),
    )
    pre_gate = jnp.einsum(
        "neci,eih->nech", rows_latent, gate_full, preferred_element_type=jnp.float32
    )
    pre_linear = jnp.einsum(
        "neci,eih->nech", rows_latent, linear_full, preferred_element_type=jnp.float32
    )
    grad_hidden = jnp.einsum(
        "necj,ehj->nech", rows_back, output_full, preferred_element_type=jnp.float32
    )
    logistic = jax.nn.sigmoid(pre_gate)
    hidden = (pre_gate * logistic * pre_linear).astype(jnp.bfloat16)
    gate_delta = (grad_hidden * pre_linear * logistic * (1.0 + pre_gate * (1.0 - logistic))).astype(
        jnp.bfloat16
    )
    linear_delta = (grad_hidden * pre_gate * logistic).astype(jnp.bfloat16)
    gate_part = jnp.einsum(
        "neci,nech->eih", rows_latent, gate_delta, preferred_element_type=jnp.float32
    )
    linear_part = jnp.einsum(
        "neci,nech->eih", rows_latent, linear_delta, preferred_element_type=jnp.float32
    )
    out_part = jnp.einsum("nech,necj->ehj", hidden, rows_back, preferred_element_type=jnp.float32)
    gate_share, linear_share, out_share = (
        lax.psum_scatter(
            gate_part.astype(jnp.bfloat16), "dp", scatter_dimension=1, tiled=True
        ).astype(jnp.float32),
        lax.psum_scatter(
            linear_part.astype(jnp.bfloat16), "dp", scatter_dimension=1, tiled=True
        ).astype(jnp.float32),
        lax.psum_scatter(
            out_part.astype(jnp.bfloat16), "dp", scatter_dimension=2, tiled=True
        ).astype(jnp.float32),
    )
    row_part = jnp.einsum(
        "nech,eih->neci", gate_delta, gate_full, preferred_element_type=jnp.float32
    )
    row_part = row_part + jnp.einsum(
        "nech,eih->neci", linear_delta, linear_full, preferred_element_type=jnp.float32
    )
    row_whole = lax.psum(row_part, "half").astype(jnp.bfloat16)
    returned = lax.all_to_all(row_whole, "expert", split_axis=0, concat_axis=0, tiled=True)
    position = expert_ids * capacity + slot_ids
    gathered = returned.reshape(expert_count * capacity, width)[position]
    latent_grad = jnp.sum(gathered.astype(jnp.float32), axis=1)
    token_grad = lax.dot_general(
        latent_grad.astype(jnp.bfloat16),
        down_full,
        (((1,), (1,)), ((), ())),
        preferred_element_type=jnp.float32,
    )
    return (
        token_grad.astype(jnp.bfloat16),
        gate_share.astype(jnp.bfloat16),
        linear_share.astype(jnp.bfloat16),
        out_share.astype(jnp.bfloat16),
    )


def solution(mesh):
    in_specs = (
        P(("expert", "dp"), "half"),
        P(("expert", "dp"), "half"),
        P(("expert", "dp"), None),
        P(("expert", "dp"), None),
        P(("expert", "dp"), None),
        P("half", "dp"),
        P("dp", "half"),
        P("expert", "dp", "half"),
        P("expert", "dp", "half"),
        P("expert", "half", "dp"),
    )
    out_specs = (
        P(("expert", "dp"), "half"),
        P("expert", "dp", "half"),
        P("expert", "dp", "half"),
        P("expert", "half", "dp"),
    )
    return jax.shard_map(
        on_device, mesh=mesh, in_specs=in_specs, out_specs=out_specs, check_vma=False
    )
```

profile of v0, /device:TPU:38, one launch (start us, length us, event | category | flops | bytes accessed | tf_op | source)
XLA Modules:
  0.0 497.7 jit_solution(3944161558312490674)
XLA Ops:
  7.2 0.7 all-gather.10.cloned.1.call-update
  8.0 0.7 all-gather.6.cloned.1.call-update
  8.7 0.1 copy.38
  8.9 0.6 fusion.2
  9.5 0.6 select_reduce_fusion
  10.1 0.1 broadcast_in_dim.37
  10.4 21.0 %all-gather.10.cloned.1.call-done = bf16[2048,1024]{1,0:T(8,128)(2,1)} async-done(((bf16[2048,512]{1,0:T(8,128)(2,1)}), bf16[2048,1024]{1,0:T(8,128)(2,1)}) %all-gather.10.cloned.1.call-update) | async-done | bytes 4194320 | tf_op jit(solution)/shard_map/all_gather | solution.py:28
  31.4 2.9 fusion.74
  34.3 18.1 %all-reduce.5 = bf16[128,1024]{1,0:T(8,128)(2,1)S(1)} all-reduce(f32[128,1024]{1,0:T(8,128)S(1)} %fusion.74), channel_id=1, replica_groups=mesh['expert'=64,'half'=2,'dp'=2] {'half'}, use_global_device_ids=true, to_apply=%region_3.4 | all-reduce | flops 131072 | bytes 786432 | tf_op jit(solution)/shard_map/psum | solution.py:38
  52.4 4.4 gather_fusion.2
  56.8 2.4 gather.20
  59.3 4.7 copy_select_fusion
  63.9 3.1 copy.46
  67.0 12.9 %all-to-all-start.1 = ((bf16[64,1,18,1024]{3,2,1,0:T(8,128)(2,1)}), bf16[64,1,18,1024]{3,2,1,0:T(8,128)(2,1)}, u32[]{:S(2)}, u32[]{:S(2)}) async-start(bf16[64,1,18,1024]{3,2,1,0:T(8,128)(2,1)} %copy.46), calls=%async_computation.1 | async-start | bytes 6291456 | tf_op jit(solution)/shard_map/all_to_all | solution.py:58
  80.0 0.2 all-reduce.4.cloned.1.call-start
  80.2 4.5 fusion.73
  85.0 4.6 gather_fusion
  89.5 0.1 mul.46
  89.7 50.7 %all-reduce.4.cloned.1.call-done = f32[128,1024]{1,0:T(8,128)} async-done(((f32[128,1024]{1,0:T(8,128)}), f32[128,1024]{1,0:T(8,128)}) %all-reduce.4.cloned.1.call-update) | async-done | bytes 524304 | tf_op jit(solution)/shard_map/psum | solution.py:38
  140.4 7.6 %gather_fusion.1 = f32[1152,1024]{1,0:T(8,128)} fusion(f32[128,1024]{1,0:T(8,128)} %all-reduce.4.cloned.1.call-done, s32[2048]{0:T(1024)S(1)} %pad_clamp_fusion), kind=kCustom, calls=%fused_computation.1 | custom fusion | bytes 9441792 | tf_op jit(solution)/shard_map/gather | solution.py:52
  148.1 5.6 %gather.18 = f32[64,1,18,1024]{3,2,0,1:T(8,128)} reshape(f32[1152,1024]{1,0:T(8,128)} %gather_fusion.1) | data formatting | bytes 9437184 | tf_op jit(solution)/shard_map/gather | solution.py:52
  153.6 5.6 %fusion.1 = bf16[64,1,18,1024]{3,0,2,1:T(8,128)(2,1)S(1)} fusion(f32[64,1,18,1024]{3,2,0,1:T(8,128)} %gather.18, f32[64,18]{0,1:T(8,128)S(1)} %copy.41, pred[64,18]{0,1:T(8,128)(4,1)S(1)} %copy.39), kind=kLoop, calls=%fused_computation.6 | loop fusion | flops 3538944 | bytes 7083648 | tf_op jit(solution)/shard_map/convert_element_type | solution.py:52
  159.3 3.0 copy.43
  162.3 10.3 %all-to-all-start = ((bf16[64,1,18,1024]{3,2,1,0:T(8,128)(2,1)}), bf16[64,1,18,1024]{3,2,1,0:T(8,128)(2,1)}, u32[]{:S(2)}, u32[]{:S(2)}) async-start(bf16[64,1,18,1024]{3,2,1,0:T(8,128)(2,1)} %copy.43), calls=%async_computation | async-start | bytes 6291456 | tf_op jit(solution)/shard_map/all_to_all | solution.py:59
  172.7 0.5 all-gather.14.cloned.1.call-update
  173.3 0.5 all-gather.12.cloned.1.call-update
  173.8 0.5 all-gather.8.cloned.1.call-update
  174.4 0.3 reduce-scatter.8.cloned.1.call-start
  174.6 16.8 %all-gather.14.cloned.1.call-done = bf16[1,1024,768]{2,1,0:T(8,128)(2,1)} async-done(((bf16[1,512,768]{2,1,0:T(8,128)(2,1)}), bf16[1,1024,768]{2,1,0:T(8,128)(2,1)}) %all-gather.14.cloned.1.call-update) | async-done | bytes 1572880 | tf_op jit(solution)/shard_map/all_gather | solution.py:30
  191.4 8.2 %fusion.17 = f32[64,18,768]{2,0,1:T(8,128)} fusion(bf16[1,1024,768]{2,1,0:T(8,128)(2,1)} %all-gather.14.cloned.1.call-done, bf16[64,1,18,1024]{3,2,1,0:T(8,128)(2,1)} %all-to-all-done.1), kind=kOutput, calls=%fused_computation.35 | convolution fusion | flops 1811939328 | bytes 7471104 | tf_op jit(solution)/shard_map/neci,eih->nech/dot_general | solution.py:61
  199.6 10.1 %all-gather.12.cloned.1.call-done = bf16[1,1024,768]{2,1,0:T(8,128)(2,1)} async-done(((bf16[1,512,768]{2,1,0:T(8,128)(2,1)}), bf16[1,1024,768]{2,1,0:T(8,128)(2,1)}) %all-gather.12.cloned.1.call-update) | async-done | bytes 1572880 | tf_op jit(solution)/shard_map/all_gather | solution.py:31
  209.7 8.2 %fusion.19 = f32[64,18,768]{2,0,1:T(8,128)} fusion(bf16[1,1024,768]{2,1,0:T(8,128)(2,1)} %all-gather.12.cloned.1.call-done, bf16[64,1,18,1024]{3,2,1,0:T(8,128)(2,1)} %all-to-all-done.1), kind=kOutput, calls=%fused_computation.37 | convolution fusion | flops 1811939328 | bytes 7471104 | tf_op jit(solution)/shard_map/neci,eih->nech/dot_general | solution.py:64
  217.9 30.1 %all-to-all-done = bf16[64,1,18,1024]{3,2,1,0:T(8,128)(2,1)} async-done(((bf16[64,1,18,1024]{3,2,1,0:T(8,128)(2,1)}), bf16[64,1,18,1024]{3,2,1,0:T(8,128)(2,1)}, u32[]{:S(2)}, u32[]{:S(2)}) %all-to-all-start) | async-done | bytes 2359328 | tf_op jit(solution)/shard_map/all_to_all | solution.py:59
  248.0 9.5 %fusion.61 = bf16[1,768,1024]{2,1,0:T(8,128)(2,1)} fusion(bf16[64,1,18,1024]{3,2,1,0:T(8,128)(2,1)} %all-to-all-done, f32[64,18,768]{2,0,1:T(8,128)} %fusion.19, f32[64,18,768]{2,0,1:T(8,128)} %fusion.17), kind=kOutput, calls=%fused_computation.60 | convolution fusion | flops 1818034176 | bytes 11010048 | tf_op jit(solution)/shard_map/nech,necj->ehj/dot_general | solution.py:82
  257.5 0.4 reduce-scatter.4.cloned.1.call-start
  258.0 9.3 %fusion.8 = (bf16[64,1,18,768]{3,0,2,1:T(8,128)(2,1)S(1)}, bf16[64,1,18,768]{3,0,2,1:T(8,128)(2,1)S(1)}) fusion(f32[64,18,768]{2,0,1:T(8,128)} %fusion.17, f32[64,18,768]{2,0,1:T(8,128)} %fusion.19, bf16[1,768,1024]{2,1,0:T(8,128)(2,1)} %all-gather.8.cloned.1.call-done, bf16[64,1,18,1024]{3,2,1,0:T(8,128)(2,1)} %all-to-all-done), kind=kOutput, calls=%fused_computation.19 | convolution fusion | flops 1823440896 | bytes 14548992 | tf_op jit(solution)/shard_map/necj,ehj->nech/dot_general | solution.py:67
  267.3 2.1 fusion.29
  269.4 4.2 add_bitcast_fusion
  273.6 6.1 %fusion.51 = bf16[1,1024,768]{2,1,0:T(8,128)(2,1)} fusion(bf16[64,1,18,768]{3,0,2,1:T(8,128)(2,1)S(1)} %get-tuple-element.9, bf16[64,1,18,1024]{3,2,1,0:T(8,128)(2,1)} %all-to-all-done.1), kind=kOutput, calls=%fused_computation.58 | convolution fusion | flops 1812725760 | bytes 5701632 | tf_op jit(solution)/shard_map/neci,nech->eih/dot_general | solution.py:76
  279.8 109.2 %all-reduce.6 = bf16[64,1,18,1024]{3,0,2,1:T(8,128)(2,1)S(1)} all-reduce(f32[64,1,18,1024]{3,0,2,1:T(8,128)} %add_bitcast_fusion), channel_id=1, replica_groups=mesh['expert'=64,'half'=2,'dp'=2] {'half'}, use_global_device_ids=true, to_apply=%region_4.5 | all-reduce | flops 1179648 | bytes 7077888 | tf_op jit(solution)/shard_map/psum | solution.py:100
  389.0 3.0 copy.48
  392.0 9.3 %all-to-all-start.2 = ((bf16[64,1,18,1024]{3,2,1,0:T(8,128)(2,1)}), bf16[64,1,18,1024]{3,2,1,0:T(8,128)(2,1)}, u32[]{:S(2)}, u32[]{:S(2)}) async-start(bf16[64,1,18,1024]{3,2,1,0:T(8,128)(2,1)} %copy.48), calls=%async_computation.2 | async-start | bytes 6291456 | tf_op jit(solution)/shard_map/all_to_all | solution.py:101
  401.4 6.0 %fusion.56 = bf16[1,1024,768]{2,1,0:T(8,128)(2,1)} fusion(bf16[64,1,18,768]{3,0,2,1:T(8,128)(2,1)S(1)} %copy-done.9, bf16[64,1,18,1024]{3,2,1,0:T(8,128)(2,1)} %all-to-all-done.1), kind=kOutput, calls=%fused_computation.59 | convolution fusion | flops 1812725760 | bytes 5701632 | tf_op jit(solution)/shard_map/neci,nech->eih/dot_general | solution.py:79
  407.6 67.5 %all-to-all-done.2 = bf16[64,1,18,1024]{3,2,1,0:T(8,128)(2,1)} async-done(((bf16[64,1,18,1024]{3,2,1,0:T(8,128)(2,1)}), bf16[64,1,18,1024]{3,2,1,0:T(8,128)(2,1)}, u32[]{:S(2)}, u32[]{:S(2)}) %all-to-all-start.2) | async-done | bytes 2359328 | tf_op jit(solution)/shard_map/all_to_all | solution.py:101
  475.1 2.9 reshape.185
  478.1 5.4 %gather_fusion.3 = bf16[1024,1024]{1,0:T(8,128)(2,1)} fusion(bf16[1152,1024]{1,0:T(8,128)(2,1)S(1)} %reshape.185, s32[1024]{0:T(1024)S(1)} %broadcast_clamp_fusion), kind=kCustom, calls=%fused_computation.3 | custom fusion | bytes 4198400 | tf_op jit(solution)/shard_map/gather | solution.py:103
  483.4 3.0 bitcast_reduce_fusion
  486.5 4.5 convolution_convert_fusion
  (48 shorter events, 1.1 us)
Async XLA Ops:
  7.2 24.3 %copy-start = (bf16[128,2048]{1,0:T(8,128)(2,1)S(1)}, bf16[128,2048]{1,0:T(8,128)(2,1)}, u32[]{:S(2)}) copy-start(bf16[128,2048]{1,0:T(8,128)(2,1)} %param.10) | copy-start | bytes 1572868
  7.2 1.5 copy-start.4
  7.2 1.5 copy-start.5
  7.2 24.2 %all-gather.10.cloned.1.call-start = ((), (), s32[]{:S(2)}) async-start(), calls=%async_computation.9 | async-start | bytes 6291456 | tf_op jit(solution)/shard_map/all_gather | solution.py:28
  7.9 72.3 %all-gather.6.cloned.1.call-start = ((), (), s32[]{:S(2)}) async-start(), calls=%async_computation.6 | async-start | bytes 6291456 | tf_op jit(solution)/shard_map/all_gather | solution.py:29
  67.0 13.2 %copy-start.2 = (bf16[128,2048]{1,0:T(8,128)(2,1)S(1)}, bf16[128,2048]{1,0:T(8,128)(2,1)}, u32[]{:S(2)}) copy-start(bf16[128,2048]{1,0:T(8,128)(2,1)} %param.11) | copy-start | bytes 1572868
  67.0 95.3 %all-to-all-start.1 = ((bf16[64,1,18,1024]{3,2,1,0:T(8,128)(2,1)}), bf16[64,1,18,1024]{3,2,1,0:T(8,128)(2,1)}, u32[]{:S(2)}, u32[]{:S(2)}) async-start(bf16[64,1,18,1024]{3,2,1,0:T(8,128)(2,1)} %copy.46), calls=%async_computation.1 | async-start | bytes 6291456 | tf_op jit(solution)/shard_map/all_to_all | solution.py:58
  79.9 4.8 copy-start.3
  80.0 60.5 %all-reduce.4.cloned.1.call-start = ((), (), s32[]{:S(2)}) async-start(), calls=%async_computation.7 | async-start | bytes 1048576 | tf_op jit(solution)/shard_map/psum | solution.py:38
  162.3 85.7 %all-to-all-start = ((bf16[64,1,18,1024]{3,2,1,0:T(8,128)(2,1)}), bf16[64,1,18,1024]{3,2,1,0:T(8,128)(2,1)}, u32[]{:S(2)}, u32[]{:S(2)}) async-start(bf16[64,1,18,1024]{3,2,1,0:T(8,128)(2,1)} %copy.43), calls=%async_computation | async-start | bytes 6291456 | tf_op jit(solution)/shard_map/all_to_all | solution.py:59
  172.6 18.8 %all-gather.14.cloned.1.call-start = ((), (), s32[]{:S(2)}) async-start(), calls=%async_computation.11 | async-start | bytes 2359296 | tf_op jit(solution)/shard_map/all_gather | solution.py:30
  173.2 36.5 %all-gather.12.cloned.1.call-start = ((), (), s32[]{:S(2)}) async-start(), calls=%async_computation.10 | async-start | bytes 2359296 | tf_op jit(solution)/shard_map/all_gather | solution.py:31
  173.8 84.2 %all-gather.8.cloned.1.call-start = ((), (), s32[]{:S(2)}) async-start(), calls=%async_computation.8 | async-start | bytes 2359296 | tf_op jit(solution)/shard_map/all_gather | solution.py:32
  174.4 316.6 %reduce-scatter.8.cloned.1.call-start = ((), (), s32[]{:S(2)}) async-start(), calls=%async_computation.14 | async-start | bytes 2359296 | tf_op jit(solution)/shard_map/reduce_scatter | solution.py:90
  257.5 9.8 %copy-start.6 = (bf16[1,1024,768]{2,1,0:T(8,128)(2,1)S(1)}, bf16[1,1024,768]{2,1,0:T(8,128)(2,1)}, u32[]{:S(2)}) copy-start(bf16[1,1024,768]{2,1,0:T(8,128)(2,1)} %all-gather.14.cloned.1.call-done) | copy-start | bytes 4718596
  257.5 233.5 %reduce-scatter.4.cloned.1.call-start = ((), (), s32[]{:S(2)}) async-start(), calls=%async_computation.12 | async-start | bytes 2359296 | tf_op jit(solution)/shard_map/reduce_scatter | solution.py:84
  267.3 2.1 copy-start.8
  267.3 2.1 copy-start.7
  392.0 9.4 %copy-start.9 = (bf16[64,1,18,768]{3,0,2,1:T(8,128)(2,1)S(1)}, bf16[64,1,18,768]{3,0,2,1:T(8,128)(2,1)}, u32[]{:S(2)}) copy-start(bf16[64,1,18,768]{3,0,2,1:T(8,128)(2,1)} %copy-done.8) | copy-start | bytes 5308420
  392.0 83.1 %all-to-all-start.2 = ((bf16[64,1,18,1024]{3,2,1,0:T(8,128)(2,1)}), bf16[64,1,18,1024]{3,2,1,0:T(8,128)(2,1)}, u32[]{:S(2)}, u32[]{:S(2)}) async-start(bf16[64,1,18,1024]{3,2,1,0:T(8,128)(2,1)} %copy.48), calls=%async_computation.2 | async-start | bytes 6291456 | tf_op jit(solution)/shard_map/all_to_all | solution.py:101
  401.3 89.7 %reduce-scatter.6.cloned.1.call-start = ((), (), s32[]{:S(2)}) async-start(), calls=%async_computation.13 | async-start | bytes 2359296 | tf_op jit(solution)/shard_map/reduce_scatter | solution.py:87
  478.1 12.9 %copy-start.1 = (bf16[128,2048]{1,0:T(8,128)(2,1)S(1)}, bf16[128,2048]{1,0:T(8,128)(2,1)}, u32[]{:S(2)}) copy-start(bf16[128,2048]{1,0:T(8,128)(2,1)} %param.10) | copy-start | bytes 1572868
Sparse Core Ops, SparseCore 0:
  9.8 21.5 all-gather.9
  33.2 20.2 all-gather.5
  84.9 55.5 all-reduce.3
  175.1 16.2 all-gather.13
  193.2 16.4 all-gather.11
  211.5 16.4 all-gather.7
  257.6 8.8 reduce-scatter.7
  279.9 8.8 reduce-scatter.3
  407.6 15.5 reduce-scatter.5
where the time goes:
time: 505 us; the launch traced here: 498 us
  waiting for transfers between devices  199 us (39%)
  blocking collectives  127 us (25%)
  matrix products  65.5 us (13%)
  local copies, waits for them, and re-layouts  43.1 us (9%)
  starting transfers between devices  33.7 us (7%)
  other arithmetic  14.6 us (3%)
  between operations  14.3 us (3%)
    psum x1, blocking collectives, on_device(): row_whole = lax.psum(row_part, 'half').astype(jnp.bfloat16)  109 us
    all_to_all x1, waiting for transfers between devices, on_device(): lax.all_to_all(row_whole, 'expert', split_axis=0, concat_axis=0, tiled=True)  67.5 us
    psum x1, waiting for transfers between devices, on_device(): latent_sum, back_latent = lax.psum((latent_part, back_part), 'half')  50.7 us
    all_to_all x1, waiting for transfers between devices, on_device(): lax.all_to_all(send_back, 'expert', split_axis=0, concat_axis=0, tiled=True)  30.1 us
    all_gather x1, waiting for transfers between devices, on_device(): lax.all_gather(latent_down, 'dp', axis=1, tiled=True)  21 us
    psum x1, blocking collectives, on_device(): latent_sum, back_latent = lax.psum((latent_part, back_part), 'half')  18.1 us
    all_gather x1, waiting for transfers between devices, on_device(): lax.all_gather(expert_gate, 'dp', axis=1, tiled=True)  16.8 us
    gather x2, local copies, waits for them, and re-layouts, on_device(): back_latent[token_of]  13.2 us
  transfers between devices with their start and end apart: 12, of which 6 were waited for; matrix products, arithmetic and copies ran while one was open for 25% of the time, Pallas kernels for 0%

commit v1 on v0

--- a/solution.py
+++ b/solution.py
@@ -2,6 +2,11 @@
 import jax.numpy as jnp
 from jax import lax
 from jax.sharding import PartitionSpec as P
+
+
+def tiled_gather(x, axis, dim):
+    copies = jnp.concatenate([x] * lax.axis_size(axis), axis=dim)
+    return lax.all_to_all(copies, axis, dim, dim, tiled=True)
 
 
 def on_device(
@@ -25,7 +30,7 @@
         row_count, 2 * ((9 * row_count * pick_count + 16 * expert_count - 1) // (16 * expert_count))
     )
     down_full, up_full, gate_full, linear_full, output_full = (
-        lax.all_gather(latent_down, "dp", axis=1, tiled=True),
+        tiled_gather(latent_down, "dp", 1),
         lax.all_gather(latent_up, "dp", axis=0, tiled=True),
         lax.all_gather(expert_gate, "dp", axis=1, tiled=True),
         lax.all_gather(expert_linear, "dp", axis=1, tiled=True),

time: 505 us -> 517 us (1.024)
  waiting for transfers between devices: 199 us -> 182 us
  local copies, waits for them, and re-layouts: 43.1 us -> 58.8 us
  starting transfers between devices: 33.7 us -> 43.5 us
    all_gather x1 -> x0, waiting for transfers between devices: 21 us -> none  [on_device(): lax.all_gather(latent_down, 'dp', axis=1, tiled=True)]
    all_to_all x0 -> x2, local copies, waits for them, and re-layouts: none -> 12.5 us  [tiled_gather(): return lax.all_to_all(copies, axis, dim, dim, tiled=True)]
    all_to_all x0 -> x1, starting transfers between devices: none -> 5.84 us  [tiled_gather(): return lax.all_to_all(copies, axis, dim, dim, tiled=True)]
  transfers between devices with their start and end apart: 12 -> 12, of which waited for: 6 -> 6; matrix products, arithmetic and copies ran while one was open for 25% -> 28% of each run, Pallas kernels for 0% -> 0%
where the time goes in v1:
time: 517 us; the launch traced here: 508 us
  waiting for transfers between devices  182 us (35%)
  blocking collectives  127 us (25%)
  matrix products  65.2 us (13%)
  local copies, waits for them, and re-layouts  58.8 us (11%)
  starting transfers between devices  43.5 us (8%)
  other arithmetic  17.1 us (3%)
  between operations  14.6 us (3%)
    psum x1, blocking collectives, on_device(): row_whole = lax.psum(row_part, 'half').astype(jnp.bfloat16)  109 us
    all_to_all x1, waiting for transfers between devices, on_device(): lax.all_to_all(row_whole, 'expert', split_axis=0, concat_axis=0, tiled=True)  67.5 us
    psum x1, waiting for transfers between devices, on_device(): latent_sum, back_latent = lax.psum((latent_part, back_part), 'half')  50.6 us
    all_to_all x1, waiting for transfers between devices, on_device(): lax.all_to_all(send_back, 'expert', split_axis=0, concat_axis=0, tiled=True)  29.8 us
    psum x1, blocking collectives, on_device(): latent_sum, back_latent = lax.psum((latent_part, back_part), 'half')  17.8 us
    all_gather x1, waiting for transfers between devices, on_device(): lax.all_gather(expert_gate, 'dp', axis=1, tiled=True)  16.9 us
    all_to_all x1, starting transfers between devices, on_device(): lax.all_to_all(send_latent, 'expert', split_axis=0, concat_axis=0, tiled=...  16.6 us
    gather x2, local copies, waits for them, and re-layouts, on_device(): back_latent[token_of]  13.3 us
  transfers between devices with their start and end apart: 12, of which 6 were waited for; matrix products, arithmetic and copies ran while one was open for 28% of the time, Pallas kernels for 0%

profile of v1, /device:TPU:38, one launch (start us, length us, event | category | flops | bytes accessed | tf_op | source)
XLA Modules:
  0.0 508.0 jit_solution(6533873796283148021)
XLA Ops:
  7.2 0.7 all-gather.5.cloned.1.call-update
  7.9 2.9 copy.66
  10.9 2.6 pad_maximum_fusion
  13.4 6.2 %copy.68 = bf16[2048,2,512]{2,0,1:T(8,128)(2,1)} copy(bf16[2048,2,512]{0,2,1:T(8,128)(2,1)} %bitcast.176) | data formatting | bytes 8388608 | tf_op jit(solution)/shard_map/all_to_all | solution.py:9
  19.6 5.8 %all-to-all-start.1 = ((bf16[2048,2,512]{2,0,1:T(8,128)(2,1)}), bf16[2048,2,512]{2,0,1:T(8,128)(2,1)}, u32[]{:S(2)}, u32[]{:S(2)}) async-start(bf16[2048,2,512]{2,0,1:T(8,128)(2,1)} %copy.68), calls=%async_computation.1 | async-start | bytes 8388608 | tf_op jit(solution)/shard_map/all_to_all | solution.py:9
  25.7 4.3 all-to-all-done.1
  30.0 6.3 %copy.69 = bf16[2048,2,512]{0,2,1:T(8,128)(2,1)} copy(bf16[2048,2,512]{2,0,1:T(8,128)(2,1)} %all-to-all-done.1) | data formatting | bytes 8388608 | tf_op jit(solution)/shard_map/all_to_all | solution.py:9
  36.2 3.4 convolution_bitcast_fusion
  39.7 17.8 %all-reduce.5 = bf16[128,1024]{0,1:T(8,128)(2,1)S(1)} all-reduce(f32[128,1024]{0,1:T(8,128)S(1)} %convolution_bitcast_fusion), channel_id=1, replica_groups=mesh['expert'=64,'half'=2,'dp'=2] {'half'}, use_global_device_ids=true, to_apply=%region_3.4 | all-reduce | flops 131072 | bytes 786432 | tf_op jit(solution)/shard_map/psum | solution.py:43
  57.5 0.6 fusion.2
  58.6 0.6 select_reduce_fusion
  59.2 4.4 gather_fusion.2
  63.6 2.4 gather.20
  66.0 4.7 copy_select_fusion
  70.7 3.1 copy.72
  73.8 16.6 %all-to-all-start.2 = ((bf16[64,1,18,1024]{3,2,1,0:T(8,128)(2,1)}), bf16[64,1,18,1024]{3,2,1,0:T(8,128)(2,1)}, u32[]{:S(2)}, u32[]{:S(2)}) async-start(bf16[64,1,18,1024]{3,2,1,0:T(8,128)(2,1)} %copy.72), calls=%async_computation.2 | async-start | bytes 6291456 | tf_op jit(solution)/shard_map/all_to_all | solution.py:63
  90.7 4.5 fusion.73
  95.4 4.6 gather_fusion
  100.2 50.6 %all-reduce.4.cloned.1.call-done = f32[128,1024]{1,0:T(8,128)} async-done(((f32[128,1024]{1,0:T(8,128)}), f32[128,1024]{1,0:T(8,128)}) %all-reduce.4.cloned.1.call-update) | async-done | bytes 524304 | tf_op jit(solution)/shard_map/psum | solution.py:43
  150.8 7.6 %gather_fusion.1 = f32[1152,1024]{1,0:T(8,128)} fusion(f32[128,1024]{1,0:T(8,128)} %all-reduce.4.cloned.1.call-done, s32[2048]{0:T(1024)S(1)} %pad_clamp_fusion), kind=kCustom, calls=%fused_computation.1 | custom fusion | bytes 9441792 | tf_op jit(solution)/shard_map/gather | solution.py:57
  158.5 5.6 %gather.18 = f32[64,1,18,1024]{3,2,0,1:T(8,128)} reshape(f32[1152,1024]{1,0:T(8,128)} %gather_fusion.1) | data formatting | bytes 9437184 | tf_op jit(solution)/shard_map/gather | solution.py:57
  164.1 5.6 %fusion.1 = bf16[64,1,18,1024]{3,0,2,1:T(8,128)(2,1)S(1)} fusion(f32[64,1,18,1024]{3,2,0,1:T(8,128)} %gather.18, f32[64,18]{0,1:T(8,128)S(1)} %copy.62, pred[64,18]{0,1:T(8,128)(4,1)S(1)} %copy.60), kind=kLoop, calls=%fused_computation.6 | loop fusion | flops 3538944 | bytes 7083648 | tf_op jit(solution)/shard_map/convert_element_type | solution.py:57
  169.8 3.0 copy.64
  172.8 10.3 %all-to-all-start = ((bf16[64,1,18,1024]{3,2,1,0:T(8,128)(2,1)}), bf16[64,1,18,1024]{3,2,1,0:T(8,128)(2,1)}, u32[]{:S(2)}, u32[]{:S(2)}) async-start(bf16[64,1,18,1024]{3,2,1,0:T(8,128)(2,1)} %copy.64), calls=%async_computation | async-start | bytes 6291456 | tf_op jit(solution)/shard_map/all_to_all | solution.py:64
  183.2 0.7 all-gather.11.cloned.1.call-update
  183.9 0.5 all-gather.9.cloned.1.call-update
  184.5 0.5 all-gather.7.cloned.1.call-update
  185.1 0.3 reduce-scatter.8.cloned.1.call-start
  185.3 16.9 %all-gather.11.cloned.1.call-done = bf16[1,1024,768]{2,1,0:T(8,128)(2,1)} async-done(((bf16[1,512,768]{2,1,0:T(8,128)(2,1)}), bf16[1,1024,768]{2,1,0:T(8,128)(2,1)}) %all-gather.11.cloned.1.call-update) | async-done | bytes 1572880 | tf_op jit(solution)/shard_map/all_gather | solution.py:35
  202.3 8.2 %fusion.17 = f32[64,18,768]{2,0,1:T(8,128)} fusion(bf16[1,1024,768]{2,1,0:T(8,128)(2,1)} %all-gather.11.cloned.1.call-done, bf16[64,1,18,1024]{3,2,1,0:T(8,128)(2,1)} %all-to-all-done.2), kind=kOutput, calls=%fused_computation.36 | convolution fusion | flops 1811939328 | bytes 7471104 | tf_op jit(solution)/shard_map/neci,eih->nech/dot_general | solution.py:66
  210.4 10.1 %all-gather.9.cloned.1.call-done = bf16[1,1024,768]{2,1,0:T(8,128)(2,1)} async-done(((bf16[1,512,768]{2,1,0:T(8,128)(2,1)}), bf16[1,1024,768]{2,1,0:T(8,128)(2,1)}) %all-gather.9.cloned.1.call-update) | async-done | bytes 1572880 | tf_op jit(solution)/shard_map/all_gather | solution.py:36
  220.5 8.2 %fusion.19 = f32[64,18,768]{2,0,1:T(8,128)} fusion(bf16[1,1024,768]{2,1,0:T(8,128)(2,1)} %all-gather.9.cloned.1.call-done, bf16[64,1,18,1024]{3,2,1,0:T(8,128)(2,1)} %all-to-all-done.2), kind=kOutput, calls=%fused_computation.38 | convolution fusion | flops 1811939328 | bytes 7471104 | tf_op jit(solution)/shard_map/neci,eih->nech/dot_general | solution.py:69
  228.7 29.8 %all-to-all-done = bf16[64,1,18,1024]{3,2,1,0:T(8,128)(2,1)} async-done(((bf16[64,1,18,1024]{3,2,1,0:T(8,128)(2,1)}), bf16[64,1,18,1024]{3,2,1,0:T(8,128)(2,1)}, u32[]{:S(2)}, u32[]{:S(2)}) %all-to-all-start) | async-done | bytes 2359328 | tf_op jit(solution)/shard_map/all_to_all | solution.py:64
  258.5 9.5 %fusion.61 = bf16[1,768,1024]{2,1,0:T(8,128)(2,1)} fusion(bf16[64,1,18,1024]{3,2,1,0:T(8,128)(2,1)} %all-to-all-done, f32[64,18,768]{2,0,1:T(8,128)} %fusion.19, f32[64,18,768]{2,0,1:T(8,128)} %fusion.17), kind=kOutput, calls=%fused_computation.61 | convolution fusion | flops 1818034176 | bytes 11010048 | tf_op jit(solution)/shard_map/nech,necj->ehj/dot_general | solution.py:87
  268.0 0.4 reduce-scatter.4.cloned.1.call-start
  268.5 9.3 %fusion.8 = (bf16[64,1,18,768]{3,0,2,1:T(8,128)(2,1)S(1)}, bf16[64,1,18,768]{3,0,2,1:T(8,128)(2,1)S(1)}) fusion(f32[64,18,768]{2,0,1:T(8,128)} %fusion.17, f32[64,18,768]{2,0,1:T(8,128)} %fusion.19, bf16[1,768,1024]{2,1,0:T(8,128)(2,1)} %all-gather.7.cloned.1.call-done, bf16[64,1,18,1024]{3,2,1,0:T(8,128)(2,1)} %all-to-all-done), kind=kOutput, calls=%fused_computation.20 | convolution fusion | flops 1823440896 | bytes 14548992 | tf_op jit(solution)/shard_map/necj,ehj->nech/dot_general | solution.py:72
  277.9 2.1 fusion.29
  280.0 4.2 add_bitcast_fusion
  284.2 6.1 %fusion.51 = bf16[1,1024,768]{2,1,0:T(8,128)(2,1)} fusion(bf16[64,1,18,768]{3,0,2,1:T(8,128)(2,1)S(1)} %get-tuple-element.9, bf16[64,1,18,1024]{3,2,1,0:T(8,128)(2,1)} %all-to-all-done.2), kind=kOutput, calls=%fused_computation.59 | convolution fusion | flops 1812725760 | bytes 5701632 | tf_op jit(solution)/shard_map/neci,nech->eih/dot_general | solution.py:81
  290.3 109.2 %all-reduce.6 = bf16[64,1,18,1024]{3,0,2,1:T(8,128)(2,1)S(1)} all-reduce(f32[64,1,18,1024]{3,0,2,1:T(8,128)} %add_bitcast_fusion), channel_id=1, replica_groups=mesh['expert'=64,'half'=2,'dp'=2] {'half'}, use_global_device_ids=true, to_apply=%region_4.5 | all-reduce | flops 1179648 | bytes 7077888 | tf_op jit(solution)/shard_map/psum | solution.py:105
  399.5 3.0 copy.74
  402.5 9.6 %all-to-all-start.3 = ((bf16[64,1,18,1024]{3,2,1,0:T(8,128)(2,1)}), bf16[64,1,18,1024]{3,2,1,0:T(8,128)(2,1)}, u32[]{:S(2)}, u32[]{:S(2)}) async-start(bf16[64,1,18,1024]{3,2,1,0:T(8,128)(2,1)} %copy.74), calls=%async_computation.3 | async-start | bytes 6291456 | tf_op jit(solution)/shard_map/all_to_all | solution.py:106
  412.2 6.0 %fusion.56 = bf16[1,1024,768]{2,1,0:T(8,128)(2,1)} fusion(bf16[64,1,18,768]{3,0,2,1:T(8,128)(2,1)S(1)} %copy-done.9, bf16[64,1,18,1024]{3,2,1,0:T(8,128)(2,1)} %all-to-all-done.2), kind=kOutput, calls=%fused_computation.60 | convolution fusion | flops 1812725760 | bytes 5701632 | tf_op jit(solution)/shard_map/neci,nech->eih/dot_general | solution.py:84
  418.4 67.5 %all-to-all-done.3 = bf16[64,1,18,1024]{3,2,1,0:T(8,128)(2,1)} async-done(((bf16[64,1,18,1024]{3,2,1,0:T(8,128)(2,1)}), bf16[64,1,18,1024]{3,2,1,0:T(8,128)(2,1)}, u32[]{:S(2)}, u32[]{:S(2)}) %all-to-all-start.3) | async-done | bytes 2359328 | tf_op jit(solution)/shard_map/all_to_all | solution.py:106
  485.9 2.9 reshape.187
  488.8 5.4 %gather_fusion.3 = bf16[1024,1024]{1,0:T(8,128)(2,1)} fusion(bf16[1152,1024]{1,0:T(8,128)(2,1)S(1)} %reshape.187, s32[1024]{0:T(1024)S(1)} %broadcast_clamp_fusion), kind=kCustom, calls=%fused_computation.3 | custom fusion | bytes 4198400 | tf_op jit(solution)/shard_map/gather | solution.py:108
  494.2 3.0 bitcast_reduce_fusion
  497.2 3.7 convolution_convert_fusion
  (52 shorter events, 1.8 us)
Async XLA Ops:
  7.2 29.1 %copy-start = (bf16[128,2048]{1,0:T(8,128)(2,1)S(1)}, bf16[128,2048]{1,0:T(8,128)(2,1)}, u32[]{:S(2)}) copy-start(bf16[128,2048]{1,0:T(8,128)(2,1)} %param.10) | copy-start | bytes 1572868
  7.2 83.5 %all-gather.5.cloned.1.call-start = ((), (), s32[]{:S(2)}) async-start(), calls=%async_computation.7 | async-start | bytes 6291456 | tf_op jit(solution)/shard_map/all_gather | solution.py:34
  19.6 5.9 %copy-start.4 = (s32[128,8]{0,1:T(8,128)S(1)}, s32[128,8]{0,1:T(8,128)}, u32[]{:S(2)}) copy-start(s32[128,8]{0,1:T(8,128)} %param.13) | copy-start | bytes 12292
  19.6 5.9 %copy-start.5 = (s32[128,8]{0,1:T(8,128)S(1)}, s32[128,8]{0,1:T(8,128)}, u32[]{:S(2)}) copy-start(s32[128,8]{0,1:T(8,128)} %param.12) | copy-start | bytes 12292
  19.6 10.3 %all-to-all-start.1 = ((bf16[2048,2,512]{2,0,1:T(8,128)(2,1)}), bf16[2048,2,512]{2,0,1:T(8,128)(2,1)}, u32[]{:S(2)}, u32[]{:S(2)}) async-start(bf16[2048,2,512]{2,0,1:T(8,128)(2,1)} %copy.68), calls=%async_computation.1 | async-start | bytes 8388608 | tf_op jit(solution)/shard_map/all_to_all | solution.py:9
  73.8 16.9 %copy-start.2 = (bf16[128,2048]{1,0:T(8,128)(2,1)S(1)}, bf16[128,2048]{1,0:T(8,128)(2,1)}, u32[]{:S(2)}) copy-start(bf16[128,2048]{1,0:T(8,128)(2,1)} %param.11) | copy-start | bytes 1572868
  73.8 99.0 %all-to-all-start.2 = ((bf16[64,1,18,1024]{3,2,1,0:T(8,128)(2,1)}), bf16[64,1,18,1024]{3,2,1,0:T(8,128)(2,1)}, u32[]{:S(2)}, u32[]{:S(2)}) async-start(bf16[64,1,18,1024]{3,2,1,0:T(8,128)(2,1)} %copy.72), calls=%async_computation.2 | async-start | bytes 6291456 | tf_op jit(solution)/shard_map/all_to_all | solution.py:63
  90.4 4.8 copy-start.3
  90.4 60.4 %all-reduce.4.cloned.1.call-start = ((), (), s32[]{:S(2)}) async-start(), calls=%async_computation.8 | async-start | bytes 1048576 | tf_op jit(solution)/shard_map/psum | solution.py:43
  172.8 85.7 %all-to-all-start = ((bf16[64,1,18,1024]{3,2,1,0:T(8,128)(2,1)}), bf16[64,1,18,1024]{3,2,1,0:T(8,128)(2,1)}, u32[]{:S(2)}, u32[]{:S(2)}) async-start(bf16[64,1,18,1024]{3,2,1,0:T(8,128)(2,1)} %copy.64), calls=%async_computation | async-start | bytes 6291456 | tf_op jit(solution)/shard_map/all_to_all | solution.py:64
  183.2 19.1 %all-gather.11.cloned.1.call-start = ((), (), s32[]{:S(2)}) async-start(), calls=%async_computation.11 | async-start | bytes 2359296 | tf_op jit(solution)/shard_map/all_gather | solution.py:35
  183.9 36.6 %all-gather.9.cloned.1.call-start = ((), (), s32[]{:S(2)}) async-start(), calls=%async_computation.10 | async-start | bytes 2359296 | tf_op jit(solution)/shard_map/all_gather | solution.py:36
  184.5 84.0 %all-gather.7.cloned.1.call-start = ((), (), s32[]{:S(2)}) async-start(), calls=%async_computation.9 | async-start | bytes 2359296 | tf_op jit(solution)/shard_map/all_gather | solution.py:37
  185.1 315.9 %reduce-scatter.8.cloned.1.call-start = ((), (), s32[]{:S(2)}) async-start(), calls=%async_computation.14 | async-start | bytes 2359296 | tf_op jit(solution)/shard_map/reduce_scatter | solution.py:95
  268.0 9.8 %copy-start.6 = (bf16[1,1024,768]{2,1,0:T(8,128)(2,1)S(1)}, bf16[1,1024,768]{2,1,0:T(8,128)(2,1)}, u32[]{:S(2)}) copy-start(bf16[1,1024,768]{2,1,0:T(8,128)(2,1)} %all-gather.11.cloned.1.call-done) | copy-start | bytes 4718596
  268.0 232.9 %reduce-scatter.4.cloned.1.call-start = ((), (), s32[]{:S(2)}) async-start(), calls=%async_computation.12 | async-start | bytes 2359296 | tf_op jit(solution)/shard_map/reduce_scatter | solution.py:89
  277.9 2.1 copy-start.8
  277.9 2.1 copy-start.7
  402.5 9.6 %copy-start.9 = (bf16[64,1,18,768]{3,0,2,1:T(8,128)(2,1)S(1)}, bf16[64,1,18,768]{3,0,2,1:T(8,128)(2,1)}, u32[]{:S(2)}) copy-start(bf16[64,1,18,768]{3,0,2,1:T(8,128)(2,1)} %copy-done.8) | copy-start | bytes 5308420
  402.5 83.4 %all-to-all-start.3 = ((bf16[64,1,18,1024]{3,2,1,0:T(8,128)(2,1)}), bf16[64,1,18,1024]{3,2,1,0:T(8,128)(2,1)}, u32[]{:S(2)}, u32[]{:S(2)}) async-start(bf16[64,1,18,1024]{3,2,1,0:T(8,128)(2,1)} %copy.74), calls=%async_computation.3 | async-start | bytes 6291456 | tf_op jit(solution)/shard_map/all_to_all | solution.py:106
  412.1 88.9 %reduce-scatter.6.cloned.1.call-start = ((), (), s32[]{:S(2)}) async-start(), calls=%async_computation.13 | async-start | bytes 2359296 | tf_op jit(solution)/shard_map/reduce_scatter | solution.py:92
  488.8 12.1 %copy-start.1 = (bf16[128,2048]{1,0:T(8,128)(2,1)S(1)}, bf16[128,2048]{1,0:T(8,128)(2,1)}, u32[]{:S(2)}) copy-start(bf16[128,2048]{1,0:T(8,128)(2,1)} %param.10) | copy-start | bytes 1572868
Sparse Core Ops, SparseCore 0:
  9.8 22.9 all-gather.4
  95.3 55.4 all-reduce.3
  185.9 16.2 all-gather.10
  204.0 16.4 all-gather.8
  222.3 16.4 all-gather.6
  268.1 8.8 reduce-scatter.7
  290.4 8.8 reduce-scatter.3
  418.3 15.5 reduce-scatter.5
